TPU v7x, 128 devices: a whole 4x4x4 slice. The times are simulated.
128 devices in a mesh: gx: 16 (over y, z_lo, core), gy: 8 (over x, z_hi).
Axes of the slice: x: 4, y: 4, z: 4 (z_hi: 2, z_lo: 2; z = z_hi * 2 + z_lo), core: 2. Of those that a mesh axis runs over, the one named last changes fastest.
Arguments:
- populations: float32 [19, 256, 256, 128], P(None, 'gx', 'gy'), may hold values from 0 to 10, as said below
- solid: int32 [256, 256, 128], P('gx', 'gy'), may hold values 0 or 1
Outputs:
- advanced: float32 [19, 256, 256, 128], P(None, 'gx', 'gy')
Inputs may be any that keep to these rules, and one draw needn't show every extreme that they name: populations are positive, each between 0.5 w_i 18 and 1.5 w_i 18.
All inputs are finite; a program needn't handle non-finite values. No bound on the sum of `solid` on one device may be relied on, other than what follows from the above.
Results may differ from a plain program's by a relative error of at most 0.0001.
Values sent between devices are 32-bit elements; how exact they have to be, the bound alone decides.
No kernel may reach another device: no remote copies, remote signals or barrier semaphores. Data moves between devices by JAX's collectives and lax.ppermute only.
A program may use at most 128 MiB of HBM per device.

v0:
```python
import jax
import jax.numpy as jnp
from jax import lax
from jax.experimental import pallas as pl
from jax.experimental.pallas import tpu as pltpu
from jax.sharding import PartitionSpec as P

ITERS = 3
NQ = 19
VEL = (
    (0, 0, 0),
    (1, 0, 0), (-1, 0, 0), (0, 1, 0), (0, -1, 0), (0, 0, 1), (0, 0, -1),
    (1, 1, 0), (-1, -1, 0), (1, -1, 0), (-1, 1, 0),
    (1, 0, 1), (-1, 0, -1), (1, 0, -1), (-1, 0, 1),
    (0, 1, 1), (0, -1, -1), (0, 1, -1), (0, -1, 1),
)
RELAX = 1.6
XP = tuple(i for i in range(NQ) if VEL[i][0] == 1)
XM = tuple(i for i in range(NQ) if VEL[i][0] == -1)
YP = tuple(i for i in range(NQ) if VEL[i][1] == 1)
YM = tuple(i for i in range(NQ) if VEL[i][1] == -1)
MARK = -float(2 ** 20)
EDGE = -1e5
FLAG_X = (0, 1, -1)


def opposite(i):
    if i == 0:
        return 0
    return i + 1 if i % 2 == 1 else i - 1


def collide(f):
    keep = 1.0 - RELAX
    d = {i: f[i] - f[i + 1] for i in range(1, NQ, 2)}
    s = [f[i] + f[i + 1] for i in range(1, NQ, 2)]
    rho = ((s[0] + s[1]) + (s[2] + s[3])) + ((s[4] + s[5]) + (s[6] + s[7])) + (s[8] + f[0])
    mx = (d[1] + d[7]) + (d[9] + d[11]) + d[13]
    my = (d[3] + d[7]) + (d[15] - d[9]) + d[17]
    mz = (d[5] + d[11]) + (d[15] - d[13]) - d[17]
    inv = 1.0 / rho
    ux, uy, uz = mx * inv, my * inv, mz * inv
    a, b, c = mx * ux, my * uy, mz * uz
    base = rho - 1.5 * ((a + b) + c)
    w0, w1, w2 = RELAX / 3.0, RELAX / 18.0, RELAX / 36.0
    post = [None] * NQ
    post[0] = keep * f[0] + w0 * base
    one, two = w1 * base, w2 * base

    def pair(i, even, odd):
        post[i] = keep * f[i] + (even + odd)
        post[i + 1] = keep * f[i + 1] + (even - odd)

    k1, o1 = 4.5 * w1, 3.0 * w1
    pair(1, one + k1 * a, o1 * mx)
    pair(3, one + k1 * b, o1 * my)
    pair(5, one + k1 * c, o1 * mz)
    k2, o2 = 4.5 * w2, 3.0 * w2
    qx, qy, qz = o2 * mx, o2 * my, o2 * mz
    ka, kb, kc = k2 * a, k2 * b, k2 * c
    kx, ky = (2.0 * k2) * mx, (2.0 * k2) * my
    for i, even, cross, p, q in (
        (7, two + (ka + kb), kx * uy, qx, qy),
        (11, two + (ka + kc), kx * uz, qx, qz),
        (15, two + (kb + kc), ky * uz, qy, qz),
    ):
        pair(i, even + cross, p + q)
        pair(i + 2, even - cross, p - q)
    return post


def send_faces(x, t, last_x, last_t, raw, xp, xm, yp, ym):
    fixed = isinstance(x, int)
    rows = pl.ds(8 * t, 8)
    if fixed and x == last_x:
        for k, v in enumerate(raw(XP)):
            xp[k, rows, :] = v
    if fixed and x == 0:
        for k, v in enumerate(raw(XM)):
            xm[k, rows, :] = v
    for side, ref, group, row in ((last_t, yp, YP, 7), (0, ym, YM, 0)):
        if t != side:
            continue
        steps = [VEL[i][0] for i in group] + list(FLAG_X)
        for k, v in enumerate(raw(group)):
            to = x + steps[k]
            if fixed and not 0 <= to <= last_x:
                continue
            ref[k, pl.ds(to, 1), :] = v[row:row + 1]


def even(axis):
    return lax.axis_index(axis) % 2 == 0


def by_edge(axis, up, down):
    first = even(axis)
    return jnp.where(first, up, down), jnp.where(first, down, up)


def columns(nx, body):
    body(0)

    def step(x, carry):
        body(x)
        return carry

    lax.fori_loop(1, nx - 1, step, 0)
    body(nx - 1)


def first_kernel(f_hbm, solid_hbm, post, x0, x1, yp, ym, xp, xm, solid, sem, solid_sem):
    nx, ny = post.shape[1], post.shape[2]
    parts = sem.shape[0]
    size = nx // parts
    flags = pltpu.make_async_copy(solid_hbm, solid, solid_sem)
    flags.start()
    copies = []
    for p in range(parts):
        at = pl.ds(p * size, size)
        copies.append(pltpu.make_async_copy(f_hbm.at[:, at], post.at[:, at], sem.at[p]))
        copies[-1].start()
    flags.wait()

    def body(x):
        for t in range(ny // 8):
            rows = pl.ds(8 * t, 8)
            f = [post[i, x, rows, :] for i in range(NQ)]
            new = collide(f)
            flag = solid[x, rows, :].astype(jnp.float32)
            blocked = flag > 0.5
            for i in range(NQ):
                post[i, x, rows, :] = jnp.where(blocked, f[i] * MARK, new[i])

            def raw(group):
                extra = [flag] * (3 if group in (YP, YM) else 1)
                return [new[i] for i in group] + extra

            send_faces(x, t, nx - 1, ny // 8 - 1, raw, xp, xm, yp, ym)

    def step(x, carry):
        body(x)
        return carry

    for p in range(parts):
        copies[p].wait()
        low, high = p * size, (p + 1) * size
        if p == 0:
            body(0)
            low = 1
        if p == parts - 1:
            high -= 1
        lax.fori_loop(low, high, step, 0)
        if p == parts - 1:
            body(nx - 1)
    order_faces(xp, xm, x0, x1)


def order_faces(xp, xm, x0, x1):
    for k in range(x0.shape[0]):
        x0[k], x1[k] = by_edge("gx", xp[k], xm[k])


def corner_kernel(yp, ym, r0, r1, y0, y1):
    nx, ny = yp.shape[1], r0.shape[1]
    row = lax.broadcasted_iota(jnp.int32, yp.shape[1:], 0)

    def filled(ref, k, group, end):
        step = VEL[group[k]][0] if k < 5 else FLAG_X[k - 5]
        cz = VEL[group[k]][2] if k < 5 else 0
        v = ref[k]
        if step == 0 or cz:
            return v
        side = XP if step == 1 else XM
        at = side.index(group[k]) if k < 5 else 5
        right, left = by_edge("gx", r0[at, end:end + 1], r1[at, end:end + 1])
        return jnp.where(row == (0 if step == 1 else nx - 1), left if step == 1 else right, v)

    for k in range(yp.shape[0]):
        y0[k], y1[k] = by_edge("gy", filled(yp, k, YP, ny - 1), filled(ym, k, YM, 0))


def mark_halos(r0, r1, s0, s1, flag_x0, flag_x1, flag_y0, flag_y1, hx, hy):
    flags = by_edge("gx", flag_x0[5], flag_x1[5])
    for k in range(5):
        values = by_edge("gx", r0[k], r1[k])
        for side in range(2):
            hx[side, k] = jnp.where(flags[1 - side] > 0.5, MARK, values[1 - side])
    for k in range(5):
        values = by_edge("gy", s0[k], s1[k])
        for side, group in enumerate((YP, YM)):
            plane = 5 + FLAG_X.index(VEL[group[k]][0])
            flag = by_edge("gy", flag_y0[plane], flag_y1[plane])[1 - side]
            hy[side, k] = jnp.where(flag > 0.5, MARK, values[1 - side])


def stream(post, hx, hy, x, t):
    nx, tiles = post.shape[1], post.shape[2] // 8
    fixed = isinstance(x, int)
    own = [post[i, x, pl.ds(8 * t, 8), :] for i in range(NQ)]
    row = lax.broadcasted_iota(jnp.int32, (8, 128), 0)
    f = [own[0]]
    for i in range(1, NQ):
        cx, cy, cz = VEL[i]
        if fixed and not 0 <= x - cx < nx:
            view = hx.at[0, XP.index(i)] if cx == 1 else hx.at[1, XM.index(i)]
        else:
            view = post.at[i, x - cx]
        if cy == 1 and t == 0:
            halo = jnp.broadcast_to(hy[0, YP.index(i), pl.ds(x, 1), :], (8, 128))
            v = jnp.where(row == 0, halo, pltpu.roll(view[pl.ds(0, 8), :], 1, 0))
        elif cy == -1 and t == tiles - 1:
            halo = jnp.broadcast_to(hy[1, YM.index(i), pl.ds(x, 1), :], (8, 128))
            v = jnp.where(row == 7, halo, pltpu.roll(view[pl.ds(8 * t, 8), :], 7, 0))
        else:
            v = view[pl.ds(8 * t - cy, 8), :]
        if cz:
            v = pltpu.roll(v, cz % 128, 1)
        f.append(jnp.where(v < EDGE, own[opposite(i)], v))
    return f, own, own[0] > EDGE


def middle_kernel(post, *refs):
    halos, (out, x0, x1, yp, ym, xp, xm, hx, hy) = refs[:8], refs[8:]
    nx, ny = post.shape[1], post.shape[2]
    mark_halos(*halos, hx, hy)

    def body(x):
        for t in range(ny // 8):
            rows = pl.ds(8 * t, 8)
            f, own, fluid = stream(post, hx, hy, x, t)
            new = collide(f)
            for i in range(NQ):
                out[i, x, rows, :] = jnp.where(fluid, new[i], own[i])
            send_faces(x, t, nx - 1, ny // 8 - 1, lambda group: [new[i] for i in group], xp, xm, yp, ym)

    columns(nx, body)
    order_faces(xp, xm, x0, x1)


def last_kernel(post, *refs):
    halos, (out_hbm, stage, hx, hy, sem) = refs[:8], refs[8:]
    nx, ny = post.shape[1], post.shape[2]
    mark_halos(*halos, hx, hy)

    def body(x):
        for t in range(ny // 8):
            f, own, fluid = stream(post, hx, hy, x, t)
            for i in range(NQ):
                stage[i, x, pl.ds(8 * t, 8), :] = jnp.where(fluid, f[i], own[i] * (1.0 / MARK))

    def step(x, carry):
        body(x)
        return carry

    parts = sem.shape[0]
    size = nx // parts
    copies = []
    for p in range(parts):
        begin, end = p * size, (p + 1) * size
        if p == 0:
            body(0)
            begin = 1
        if p == parts - 1:
            end -= 1
        lax.fori_loop(begin, end, step, 0)
        if p == parts - 1:
            body(nx - 1)
        at = pl.ds(p * size, size)
        copies.append(pltpu.make_async_copy(stage.at[:, at], out_hbm.at[:, at], sem.at[p]))
        copies[-1].start()
    for copy in copies:
        copy.wait()


def swap(value, axis, edge):
    count = lax.axis_size(axis)
    pairs = [((2 * j + edge) % count, (2 * j + edge + 1) % count) for j in range(count // 2)]
    return lax.ppermute(value, axis, pairs + [(b, a) for a, b in pairs])


def local(populations, solid):
    _, nx, ny, nz = populations.shape
    f32 = jnp.float32
    anywhere = pl.BlockSpec(memory_space=pl.ANY)
    onchip = pl.BlockSpec(memory_space=pltpu.VMEM)
    state = pltpu.VMEM(populations.shape, f32)
    params = pltpu.CompilerParams(vmem_limit_bytes=24 << 20)

    def faces(x_planes, y_planes):
        shape_x = jax.ShapeDtypeStruct((x_planes, ny, nz), f32)
        shape_y = jax.ShapeDtypeStruct((y_planes, nx, nz), f32)
        return (shape_x, shape_x, shape_y, shape_y)

    def exchange(x0, x1, yp, ym):
        r0, r1 = swap(x0, "gx", 0), swap(x1, "gx", 1)
        shape = jax.ShapeDtypeStruct(yp.shape, f32)
        y0, y1 = pl.pallas_call(
            corner_kernel,
            out_shape=(shape, shape),
            in_specs=[onchip] * 4,
            out_specs=(onchip,) * 2,
            compiler_params=params,
            name="corners",
        )(yp, ym, r0, r1)
        return r0, r1, swap(y0, "gy", 0), swap(y1, "gy", 1)

    post, *out = pl.pallas_call(
        first_kernel,
        out_shape=(state,) + faces(6, 8),
        in_specs=[anywhere, anywhere],
        out_specs=(onchip,) * 5,
        scratch_shapes=[pltpu.VMEM((6, ny, nz), f32)] * 2 + [
            pltpu.VMEM(solid.shape, jnp.int32),
            pltpu.SemaphoreType.DMA((4,)),
            pltpu.SemaphoreType.DMA,
        ],
        compiler_params=params,
        name="first",
    )(
        pltpu.with_memory_space_constraint(populations, pltpu.HBM),
        pltpu.with_memory_space_constraint(solid, pltpu.HBM),
    )
    halos = exchange(*out)
    flags = halos
    marked = [pltpu.VMEM((2, 5, ny, nz), f32), pltpu.VMEM((2, 5, nx, nz), f32)]
    for _ in range(ITERS - 1):
        post = pltpu.with_memory_space_constraint(post, pltpu.VMEM)
        post, *out = pl.pallas_call(
            middle_kernel,
            out_shape=(state,) + faces(5, 5),
            in_specs=[onchip] * 9,
            out_specs=(onchip,) * 5,
            scratch_shapes=[pltpu.VMEM((5, ny, nz), f32)] * 2 + marked,
            compiler_params=params,
            name="middle",
        )(post, *halos, *flags)
        halos = exchange(*out)
    post = pltpu.with_memory_space_constraint(post, pltpu.VMEM)
    return pl.pallas_call(
        last_kernel,
        out_shape=jax.ShapeDtypeStruct(populations.shape, f32),
        in_specs=[onchip] * 9,
        out_specs=anywhere,
        scratch_shapes=[pltpu.VMEM(populations.shape, f32)] + marked + [pltpu.SemaphoreType.DMA((4,))],
        compiler_params=params,
        name="last",
    )(post, *halos, *flags)


def solution(mesh):
    in_specs = (P(None, "gx", "gy", None), P("gx", "gy", None))
    out_specs = P(None, "gx", "gy", None)
    return jax.shard_map(local, mesh=mesh, in_specs=in_specs, out_specs=out_specs, check_vma=False)
```

profile of v0, /device:TPU:0, one launch (start us, length us, event | category | flops | bytes accessed | tf_op | source)
XLA Modules:
  0.0 62.6 jit_solution(5394571175628410102)
XLA Ops:
  0.0 4.3 %first.1 = (f32[19,16,32,128]{3,2,1,0:T(8,128)S(1)}, f32[6,32,128]{2,1,0:T(8,128)S(1)}, f32[6,32,128]{2,1,0:T(8,128)S(1)}, f32[8,16,128]{2,1,0:T(8,128)S(1)}, f32[8,16,128]{2,1,0:T(8,128)S(1)}) custom-call(f32[19,16,32,128]{3,2,1,0:T(8,128)} %f_hbm.1, s32[16,32,128]{2,1,0:T(8,128)} %solid_hbm.1), custom_call_target="tpu_custom_call" | custom-call | tf_op jit(solution)/shard_map/first/pallas_call | solution.py:308
  4.3 0.1 collective-permute-start
  4.4 4.6 %collective-permute-start.1 = (f32[6,32,128]{2,1,0:T(8,128)S(1)}, f32[6,32,128]{2,1,0:T(8,128)S(1)}, u32[]{:S(2)}, u32[]{:S(2)}) collective-permute-start(f32[6,32,128]{2,1,0:T(8,128)S(1)} %get-tuple-element.28), channel_id=1, source_target_pairs={{8,16},{24,32},{40,48},{56,64},{72,80},{88,96},{104,112},{120,0},{... | collective-permute-start | bytes 294920 | tf_op jit(solution)/shard_map/ppermute | solution.py:279
  8.9 0.0 collective-permute-done.r0.refs_0_.refs_4_
  8.9 2.3 %collective-permute-done.1.r1.refs_1_.refs_5_ = f32[6,32,128]{2,1,0:T(8,128)S(1)} collective-permute-done((f32[6,32,128]{2,1,0:T(8,128)S(1)}, f32[6,32,128]{2,1,0:T(8,128)S(1)}, u32[]{:S(2)}, u32[]{:S(2)}) %collective-permute-start.1) | collective-permute-done | bytes 98336 | tf_op jit(solution)/shard_map/ppermute | solution.py:279
  11.3 3.7 %collective-permute-start.2 = (f32[8,16,128]{2,1,0:T(8,128)S(1)}, f32[8,16,128]{2,1,0:T(8,128)S(1)}, u32[]{:S(2)}, u32[]{:S(2)}) collective-permute-start(f32[8,16,128]{2,1,0:T(8,128)S(1)} %get-tuple-element.31), channel_id=1, source_target_pairs={{0,1},{2,3},{4,5},{6,7},{1,0},{3,2},{5,4},{7,6},{8,9},{10,11},{12,... | collective-permute-start | bytes 196616 | tf_op jit(solution)/shard_map/ppermute | solution.py:279
  14.9 2.3 %collective-permute-start.3 = (f32[8,16,128]{2,1,0:T(8,128)S(1)}, f32[8,16,128]{2,1,0:T(8,128)S(1)}, u32[]{:S(2)}, u32[]{:S(2)}) collective-permute-start(f32[8,16,128]{2,1,0:T(8,128)S(1)} %get-tuple-element.32), channel_id=1, source_target_pairs={{1,2},{3,4},{5,6},{7,0},{2,1},{4,3},{6,5},{0,7},{9,10},{11,12},{13... | collective-permute-start | bytes 196616 | tf_op jit(solution)/shard_map/ppermute | solution.py:279
  17.2 0.0 collective-permute-done.2.refs_2_.refs_6_
  17.2 5.6 %collective-permute-done.3.refs_3_.refs_7_ = f32[8,16,128]{2,1,0:T(8,128)S(1)} collective-permute-done((f32[8,16,128]{2,1,0:T(8,128)S(1)}, f32[8,16,128]{2,1,0:T(8,128)S(1)}, u32[]{:S(2)}, u32[]{:S(2)}) %collective-permute-start.3) | collective-permute-done | bytes 65568 | tf_op jit(solution)/shard_map/ppermute | solution.py:279
  22.8 3.4 %middle.2 = (f32[19,16,32,128]{3,2,1,0:T(8,128)S(1)}, f32[5,32,128]{2,1,0:T(8,128)S(1)}, f32[5,32,128]{2,1,0:T(8,128)S(1)}, f32[5,16,128]{2,1,0:T(8,128)S(1)}, f32[5,16,128]{2,1,0:T(8,128)S(1)}) custom-call(f32[19,16,32,128]{3,2,1,0:T(8,128)S(1)} %get-tuple-element.26.post, f32[6,32,128]{2,1,0:T(8,128)S(1)} %collective-permute-done.r0.refs_0_.refs_4_, ...), custom_call_target="tpu_custom_call" | custom-call | tf_op jit(solution)/shard_map/middle/pallas_call | solution.py:329
  26.2 0.1 collective-permute-start.4
  26.3 1.9 %collective-permute-start.5 = (f32[5,32,128]{2,1,0:T(8,128)S(1)}, f32[5,32,128]{2,1,0:T(8,128)S(1)}, u32[]{:S(2)}, u32[]{:S(2)}) collective-permute-start(f32[5,32,128]{2,1,0:T(8,128)S(1)} %get-tuple-element.35), channel_id=1, source_target_pairs={{8,16},{24,32},{40,48},{56,64},{72,80},{88,96},{104,112},{120,0},{... | collective-permute-start | bytes 245768 | tf_op jit(solution)/shard_map/ppermute | solution.py:279
  28.2 0.0 collective-permute-done.4.r0.refs_0_
  28.2 4.2 %collective-permute-done.5.r1.refs_1_ = f32[5,32,128]{2,1,0:T(8,128)S(1)} collective-permute-done((f32[5,32,128]{2,1,0:T(8,128)S(1)}, f32[5,32,128]{2,1,0:T(8,128)S(1)}, u32[]{:S(2)}, u32[]{:S(2)}) %collective-permute-start.5) | collective-permute-done | bytes 81952 | tf_op jit(solution)/shard_map/ppermute | solution.py:279
  32.4 0.1 collective-permute-start.6
  32.5 4.5 %collective-permute-start.7 = (f32[5,16,128]{2,1,0:T(8,128)S(1)}, f32[5,16,128]{2,1,0:T(8,128)S(1)}, u32[]{:S(2)}, u32[]{:S(2)}) collective-permute-start(f32[5,16,128]{2,1,0:T(8,128)S(1)} %get-tuple-element.39), channel_id=1, source_target_pairs={{1,2},{3,4},{5,6},{7,0},{2,1},{4,3},{6,5},{0,7},{9,10},{11,12},{13... | collective-permute-start | bytes 122888 | tf_op jit(solution)/shard_map/ppermute | solution.py:279
  37.0 1.0 %collective-permute-done.6.refs_2_ = f32[5,16,128]{2,1,0:T(8,128)S(1)} collective-permute-done((f32[5,16,128]{2,1,0:T(8,128)S(1)}, f32[5,16,128]{2,1,0:T(8,128)S(1)}, u32[]{:S(2)}, u32[]{:S(2)}) %collective-permute-start.6) | collective-permute-done | bytes 40992 | tf_op jit(solution)/shard_map/ppermute | solution.py:279
  38.0 2.2 %collective-permute-done.7.refs_3_ = f32[5,16,128]{2,1,0:T(8,128)S(1)} collective-permute-done((f32[5,16,128]{2,1,0:T(8,128)S(1)}, f32[5,16,128]{2,1,0:T(8,128)S(1)}, u32[]{:S(2)}, u32[]{:S(2)}) %collective-permute-start.7) | collective-permute-done | bytes 40992 | tf_op jit(solution)/shard_map/ppermute | solution.py:279
  40.2 3.3 %middle.3 = (f32[19,16,32,128]{3,2,1,0:T(8,128)S(1)}, f32[5,32,128]{2,1,0:T(8,128)S(1)}, f32[5,32,128]{2,1,0:T(8,128)S(1)}, f32[5,16,128]{2,1,0:T(8,128)S(1)}, f32[5,16,128]{2,1,0:T(8,128)S(1)}) custom-call(f32[19,16,32,128]{3,2,1,0:T(8,128)S(1)} %get-tuple-element.33.post, f32[5,32,128]{2,1,0:T(8,128)S(1)} %collective-permute-done.4.r0.refs_0_, ...), custom_call_target="tpu_custom_call" | custom-call | tf_op jit(solution)/shard_map/middle/pallas_call | solution.py:329
  43.5 0.1 collective-permute-start.8
  43.6 0.7 %collective-permute-start.9 = (f32[5,32,128]{2,1,0:T(8,128)S(1)}, f32[5,32,128]{2,1,0:T(8,128)S(1)}, u32[]{:S(2)}, u32[]{:S(2)}) collective-permute-start(f32[5,32,128]{2,1,0:T(8,128)S(1)} %get-tuple-element.42), channel_id=1, source_target_pairs={{8,16},{24,32},{40,48},{56,64},{72,80},{88,96},{104,112},{120,0},{... | collective-permute-start | bytes 245768 | tf_op jit(solution)/shard_map/ppermute | solution.py:279
  44.3 0.6 collective-permute-done.8.r0.refs_0_
  44.8 4.8 %collective-permute-done.9.r1.refs_1_ = f32[5,32,128]{2,1,0:T(8,128)S(1)} collective-permute-done((f32[5,32,128]{2,1,0:T(8,128)S(1)}, f32[5,32,128]{2,1,0:T(8,128)S(1)}, u32[]{:S(2)}, u32[]{:S(2)}) %collective-permute-start.9) | collective-permute-done | bytes 81952 | tf_op jit(solution)/shard_map/ppermute | solution.py:279
  49.7 2.3 %collective-permute-start.10 = (f32[5,16,128]{2,1,0:T(8,128)S(1)}, f32[5,16,128]{2,1,0:T(8,128)S(1)}, u32[]{:S(2)}, u32[]{:S(2)}) collective-permute-start(f32[5,16,128]{2,1,0:T(8,128)S(1)} %get-tuple-element.45), channel_id=1, source_target_pairs={{0,1},{2,3},{4,5},{6,7},{1,0},{3,2},{5,4},{7,6},{8,9},{10,11},{12,... | collective-permute-start | bytes 122888 | tf_op jit(solution)/shard_map/ppermute | solution.py:279
  52.0 2.3 %collective-permute-start.11 = (f32[5,16,128]{2,1,0:T(8,128)S(1)}, f32[5,16,128]{2,1,0:T(8,128)S(1)}, u32[]{:S(2)}, u32[]{:S(2)}) collective-permute-start(f32[5,16,128]{2,1,0:T(8,128)S(1)} %get-tuple-element.46), channel_id=1, source_target_pairs={{1,2},{3,4},{5,6},{7,0},{2,1},{4,3},{6,5},{0,7},{9,10},{11,12},{13... | collective-permute-start | bytes 122888 | tf_op jit(solution)/shard_map/ppermute | solution.py:279
  54.2 1.0 %collective-permute-done.10.refs_2_ = f32[5,16,128]{2,1,0:T(8,128)S(1)} collective-permute-done((f32[5,16,128]{2,1,0:T(8,128)S(1)}, f32[5,16,128]{2,1,0:T(8,128)S(1)}, u32[]{:S(2)}, u32[]{:S(2)}) %collective-permute-start.10) | collective-permute-done | bytes 40992 | tf_op jit(solution)/shard_map/ppermute | solution.py:279
  55.2 4.3 %collective-permute-done.11.refs_3_ = f32[5,16,128]{2,1,0:T(8,128)S(1)} collective-permute-done((f32[5,16,128]{2,1,0:T(8,128)S(1)}, f32[5,16,128]{2,1,0:T(8,128)S(1)}, u32[]{:S(2)}, u32[]{:S(2)}) %collective-permute-start.11) | collective-permute-done | bytes 40992 | tf_op jit(solution)/shard_map/ppermute | solution.py:279
  59.6 3.0 %last.1 = f32[19,16,32,128]{3,2,1,0:T(8,128)} custom-call(f32[19,16,32,128]{3,2,1,0:T(8,128)S(1)} %get-tuple-element.40.post, f32[5,32,128]{2,1,0:T(8,128)S(1)} %collective-permute-done.8.r0.refs_0_, f32[5,32,128]{2,1,0:T(8,128)S(1)} %collective-permute-done.9.r1.refs_1_, f32[5,16,128]{2,1,0:T(8,128)S(1)} %collective-permute-done.10.refs_2_, ...), custom_call_target="tpu_custom_call" | custom-call | tf_op jit(solution)/shard_map/last/pallas_call | solution.py:340
  (3 shorter events, 0.1 us)
Async XLA Ops:
  4.3 4.7 %collective-permute-start = (f32[6,32,128]{2,1,0:T(8,128)S(1)}, f32[6,32,128]{2,1,0:T(8,128)S(1)}, u32[]{:S(2)}, u32[]{:S(2)}) collective-permute-start(f32[6,32,128]{2,1,0:T(8,128)S(1)} %get-tuple-element.27), channel_id=1, source_target_pairs={{0,8},{16,24},{32,40},{48,56},{64,72},{80,88},{96,104},{112,120},{... | collective-permute-start | bytes 294920 | tf_op jit(solution)/shard_map/ppermute | solution.py:279
  4.4 6.9 %collective-permute-start.1 = (f32[6,32,128]{2,1,0:T(8,128)S(1)}, f32[6,32,128]{2,1,0:T(8,128)S(1)}, u32[]{:S(2)}, u32[]{:S(2)}) collective-permute-start(f32[6,32,128]{2,1,0:T(8,128)S(1)} %get-tuple-element.28), channel_id=1, source_target_pairs={{8,16},{24,32},{40,48},{56,64},{72,80},{88,96},{104,112},{120,0},{... | collective-permute-start | bytes 294920 | tf_op jit(solution)/shard_map/ppermute | solution.py:279
  11.3 6.0 %collective-permute-start.2 = (f32[8,16,128]{2,1,0:T(8,128)S(1)}, f32[8,16,128]{2,1,0:T(8,128)S(1)}, u32[]{:S(2)}, u32[]{:S(2)}) collective-permute-start(f32[8,16,128]{2,1,0:T(8,128)S(1)} %get-tuple-element.31), channel_id=1, source_target_pairs={{0,1},{2,3},{4,5},{6,7},{1,0},{3,2},{5,4},{7,6},{8,9},{10,11},{12,... | collective-permute-start | bytes 196616 | tf_op jit(solution)/shard_map/ppermute | solution.py:279
  14.9 7.9 %collective-permute-start.3 = (f32[8,16,128]{2,1,0:T(8,128)S(1)}, f32[8,16,128]{2,1,0:T(8,128)S(1)}, u32[]{:S(2)}, u32[]{:S(2)}) collective-permute-start(f32[8,16,128]{2,1,0:T(8,128)S(1)} %get-tuple-element.32), channel_id=1, source_target_pairs={{1,2},{3,4},{5,6},{7,0},{2,1},{4,3},{6,5},{0,7},{9,10},{11,12},{13... | collective-permute-start | bytes 196616 | tf_op jit(solution)/shard_map/ppermute | solution.py:279
  26.2 2.0 %collective-permute-start.4 = (f32[5,32,128]{2,1,0:T(8,128)S(1)}, f32[5,32,128]{2,1,0:T(8,128)S(1)}, u32[]{:S(2)}, u32[]{:S(2)}) collective-permute-start(f32[5,32,128]{2,1,0:T(8,128)S(1)} %get-tuple-element.34), channel_id=1, source_target_pairs={{0,8},{16,24},{32,40},{48,56},{64,72},{80,88},{96,104},{112,120},{... | collective-permute-start | bytes 245768 | tf_op jit(solution)/shard_map/ppermute | solution.py:279
  26.3 6.1 %collective-permute-start.5 = (f32[5,32,128]{2,1,0:T(8,128)S(1)}, f32[5,32,128]{2,1,0:T(8,128)S(1)}, u32[]{:S(2)}, u32[]{:S(2)}) collective-permute-start(f32[5,32,128]{2,1,0:T(8,128)S(1)} %get-tuple-element.35), channel_id=1, source_target_pairs={{8,16},{24,32},{40,48},{56,64},{72,80},{88,96},{104,112},{120,0},{... | collective-permute-start | bytes 245768 | tf_op jit(solution)/shard_map/ppermute | solution.py:279
  32.4 5.6 %collective-permute-start.6 = (f32[5,16,128]{2,1,0:T(8,128)S(1)}, f32[5,16,128]{2,1,0:T(8,128)S(1)}, u32[]{:S(2)}, u32[]{:S(2)}) collective-permute-start(f32[5,16,128]{2,1,0:T(8,128)S(1)} %get-tuple-element.38), channel_id=1, source_target_pairs={{0,1},{2,3},{4,5},{6,7},{1,0},{3,2},{5,4},{7,6},{8,9},{10,11},{12,... | collective-permute-start | bytes 122888 | tf_op jit(solution)/shard_map/ppermute | solution.py:279
  32.5 7.7 %collective-permute-start.7 = (f32[5,16,128]{2,1,0:T(8,128)S(1)}, f32[5,16,128]{2,1,0:T(8,128)S(1)}, u32[]{:S(2)}, u32[]{:S(2)}) collective-permute-start(f32[5,16,128]{2,1,0:T(8,128)S(1)} %get-tuple-element.39), channel_id=1, source_target_pairs={{1,2},{3,4},{5,6},{7,0},{2,1},{4,3},{6,5},{0,7},{9,10},{11,12},{13... | collective-permute-start | bytes 122888 | tf_op jit(solution)/shard_map/ppermute | solution.py:279
  43.5 1.4 %collective-permute-start.8 = (f32[5,32,128]{2,1,0:T(8,128)S(1)}, f32[5,32,128]{2,1,0:T(8,128)S(1)}, u32[]{:S(2)}, u32[]{:S(2)}) collective-permute-start(f32[5,32,128]{2,1,0:T(8,128)S(1)} %get-tuple-element.41), channel_id=1, source_target_pairs={{0,8},{16,24},{32,40},{48,56},{64,72},{80,88},{96,104},{112,120},{... | collective-permute-start | bytes 245768 | tf_op jit(solution)/shard_map/ppermute | solution.py:279
  43.6 6.1 %collective-permute-start.9 = (f32[5,32,128]{2,1,0:T(8,128)S(1)}, f32[5,32,128]{2,1,0:T(8,128)S(1)}, u32[]{:S(2)}, u32[]{:S(2)}) collective-permute-start(f32[5,32,128]{2,1,0:T(8,128)S(1)} %get-tuple-element.42), channel_id=1, source_target_pairs={{8,16},{24,32},{40,48},{56,64},{72,80},{88,96},{104,112},{120,0},{... | collective-permute-start | bytes 245768 | tf_op jit(solution)/shard_map/ppermute | solution.py:279
  49.7 5.6 %collective-permute-start.10 = (f32[5,16,128]{2,1,0:T(8,128)S(1)}, f32[5,16,128]{2,1,0:T(8,128)S(1)}, u32[]{:S(2)}, u32[]{:S(2)}) collective-permute-start(f32[5,16,128]{2,1,0:T(8,128)S(1)} %get-tuple-element.45), channel_id=1, source_target_pairs={{0,1},{2,3},{4,5},{6,7},{1,0},{3,2},{5,4},{7,6},{8,9},{10,11},{12,... | collective-permute-start | bytes 122888 | tf_op jit(solution)/shard_map/ppermute | solution.py:279
  52.0 7.6 %collective-permute-start.11 = (f32[5,16,128]{2,1,0:T(8,128)S(1)}, f32[5,16,128]{2,1,0:T(8,128)S(1)}, u32[]{:S(2)}, u32[]{:S(2)}) collective-permute-start(f32[5,16,128]{2,1,0:T(8,128)S(1)} %get-tuple-element.46), channel_id=1, source_target_pairs={{1,2},{3,4},{5,6},{7,0},{2,1},{4,3},{6,5},{0,7},{9,10},{11,12},{13... | collective-permute-start | bytes 122888 | tf_op jit(solution)/shard_map/ppermute | solution.py:279
where the time goes:
time: 62.7 us; the launch traced here: 62.6 us
  waiting for transfers between devices  26 us (41%)
  starting transfers between devices  22.5 us (36%)
  Pallas kernels  14 us (22%)
    ppermute x12, waiting for transfers between devices, swap(): return lax.ppermute(value, axis, pairs + [(b, a) for a, b in pairs])  26 us
    ppermute x12, starting transfers between devices, swap(): return lax.ppermute(value, axis, pairs + [(b, a) for a, b in pairs])  22.5 us
    pallas_call x2, Pallas kernels, local(): pl.pallas_call(middle_kernel, out_shape=(state,) + faces(5, 5), in_specs=...  6.65 us
    pallas_call x1, Pallas kernels, local(): pl.pallas_call(first_kernel, out_shape=(state,) + faces(6, 8), in_specs=[...  4.26 us
    pallas_call x1, Pallas kernels, local(): pl.pallas_call(last_kernel, out_shape=jax.ShapeDtypeStruct(populations.sh...  2.99 us
  transfers between devices with their start and end apart: 12, of which 9 were waited for; matrix products, arithmetic and copies ran while one was open for 0% of the time, Pallas kernels for 0%

commit v1 on v0

--- a/solution.py
+++ b/solution.py
@@ -98,67 +98,61 @@
     return jnp.where(first, up, down), jnp.where(first, down, up)
 
 
-def columns(nx, body):
-    body(0)
-
+def inner_columns(nx, body):
     def step(x, carry):
         body(x)
         return carry
 
     lax.fori_loop(1, nx - 1, step, 0)
-    body(nx - 1)
-
-
-def first_kernel(f_hbm, solid_hbm, post, x0, x1, yp, ym, xp, xm, solid, sem, solid_sem):
-    nx, ny = post.shape[1], post.shape[2]
-    parts = sem.shape[0]
-    size = nx // parts
-    flags = pltpu.make_async_copy(solid_hbm, solid, solid_sem)
-    flags.start()
-    copies = []
-    for p in range(parts):
-        at = pl.ds(p * size, size)
-        copies.append(pltpu.make_async_copy(f_hbm.at[:, at], post.at[:, at], sem.at[p]))
-        copies[-1].start()
-    flags.wait()
-
-    def body(x):
-        for t in range(ny // 8):
-            rows = pl.ds(8 * t, 8)
-            f = [post[i, x, rows, :] for i in range(NQ)]
-            new = collide(f)
-            flag = solid[x, rows, :].astype(jnp.float32)
-            blocked = flag > 0.5
-            for i in range(NQ):
-                post[i, x, rows, :] = jnp.where(blocked, f[i] * MARK, new[i])
-
-            def raw(group):
-                extra = [flag] * (3 if group in (YP, YM) else 1)
-                return [new[i] for i in group] + extra
-
-            send_faces(x, t, nx - 1, ny // 8 - 1, raw, xp, xm, yp, ym)
-
-    def step(x, carry):
-        body(x)
-        return carry
-
-    for p in range(parts):
-        copies[p].wait()
-        low, high = p * size, (p + 1) * size
-        if p == 0:
-            body(0)
-            low = 1
-        if p == parts - 1:
-            high -= 1
-        lax.fori_loop(low, high, step, 0)
-        if p == parts - 1:
-            body(nx - 1)
-    order_faces(xp, xm, x0, x1)
 
 
 def order_faces(xp, xm, x0, x1):
     for k in range(x0.shape[0]):
         x0[k], x1[k] = by_edge("gx", xp[k], xm[k])
+
+
+def begin(x, t, f, solid, post, faces):
+    nx, tiles = post.shape[1], post.shape[2] // 8
+    rows = pl.ds(8 * t, 8)
+    new = collide(f)
+    flag = solid[x, rows, :].astype(jnp.float32)
+    blocked = flag > 0.5
+    for i in range(NQ):
+        post[i, x, rows, :] = jnp.where(blocked, f[i] * MARK, new[i])
+
+    def raw(group):
+        return [new[i] for i in group] + [flag] * (3 if group in (YP, YM) else 1)
+
+    send_faces(x, t, nx - 1, tiles - 1, raw, *faces)
+
+
+def first_edge_kernel(f_hbm, solid_hbm, post, x0, x1, yp, ym, xp, xm, solid, sem):
+    nx, ny = post.shape[1], post.shape[2]
+    copies = []
+    for n, x in enumerate((0, nx - 1)):
+        at = pl.ds(x, 1)
+        copies.append(pltpu.make_async_copy(solid_hbm.at[at], solid.at[at], sem.at[n]))
+        copies.append(pltpu.make_async_copy(f_hbm.at[:, at], post.at[:, at], sem.at[2 + n]))
+    for copy in copies:
+        copy.start()
+    for n, x in enumerate((0, nx - 1)):
+        copies[2 * n].wait()
+        copies[2 * n + 1].wait()
+        for t in range(ny // 8):
+            f = [post[i, x, pl.ds(8 * t, 8), :] for i in range(NQ)]
+            begin(x, t, f, solid, post, (xp, xm, yp, ym))
+    order_faces(xp, xm, x0, x1)
+
+
+def first_inner_kernel(f_ref, solid, post_in, yp_in, ym_in, post, yp, ym):
+    nx, ny = post.shape[1], post.shape[2]
+
+    def body(x):
+        for t in range(ny // 8):
+            f = [f_ref[i, x, pl.ds(8 * t, 8), :] for i in range(NQ)]
+            begin(x, t, f, solid, post, (None, None, yp, ym))
+
+    inner_columns(nx, body)
 
 
 def corner_kernel(yp, ym, r0, r1, y0, y1):
@@ -220,55 +214,96 @@
     return f, own, own[0] > EDGE
 
 
-def middle_kernel(post, *refs):
-    halos, (out, x0, x1, yp, ym, xp, xm, hx, hy) = refs[:8], refs[8:]
+def advance(post, hx, hy, x, t, out, faces):
+    nx, tiles = post.shape[1], post.shape[2] // 8
+    f, own, fluid = stream(post, hx, hy, x, t)
+    new = collide(f)
+    for i in range(NQ):
+        out[i, x, pl.ds(8 * t, 8), :] = jnp.where(fluid, new[i], own[i])
+    send_faces(x, t, nx - 1, tiles - 1, lambda group: [new[i] for i in group], *faces)
+
+
+def centre_kernel(post, out):
+    def body(x):
+        for t in range(1, post.shape[2] // 8 - 1):
+            advance(post, None, None, x, t, out, (None,) * 4)
+
+    inner_columns(post.shape[1], body)
+
+
+def edge_kernel(post, *refs):
+    halos, (out_in, out, x0, x1, yp, ym, hy, xp, xm, hx) = refs[:8], refs[8:]
     nx, ny = post.shape[1], post.shape[2]
     mark_halos(*halos, hx, hy)
-
+    for x in (0, nx - 1):
+        for t in range(ny // 8):
+            advance(post, hx, hy, x, t, out, (xp, xm, yp, ym))
+    order_faces(xp, xm, x0, x1)
+
+
+def rim_kernel(post, hy, out_in, yp_in, ym_in, out, yp, ym):
     def body(x):
-        for t in range(ny // 8):
-            rows = pl.ds(8 * t, 8)
-            f, own, fluid = stream(post, hx, hy, x, t)
-            new = collide(f)
-            for i in range(NQ):
-                out[i, x, rows, :] = jnp.where(fluid, new[i], own[i])
-            send_faces(x, t, nx - 1, ny // 8 - 1, lambda group: [new[i] for i in group], xp, xm, yp, ym)
-
-    columns(nx, body)
-    order_faces(xp, xm, x0, x1)
+        for t in (0, post.shape[2] // 8 - 1):
+            advance(post, None, hy, x, t, out, (None, None, yp, ym))
+
+    inner_columns(post.shape[1], body)
+
+
+def finish(post, hx, hy, x, t, stage):
+    f, own, fluid = stream(post, hx, hy, x, t)
+    for i in range(NQ):
+        stage[i, x, pl.ds(8 * t, 8), :] = jnp.where(fluid, f[i], own[i] * (1.0 / MARK))
+
+
+def send_out(stage, out_hbm, sem, x, nx, y, ny):
+    copy = pltpu.make_async_copy(
+        stage.at[:, pl.ds(x, nx), pl.ds(y, ny)], out_hbm.at[:, pl.ds(x, nx), pl.ds(y, ny)], sem
+    )
+    copy.start()
+    return copy
+
+
+def last_centre_kernel(post, out_hbm, stage, sem):
+    nx, ny = post.shape[1], post.shape[2]
+    parts = sem.shape[0]
+    size = (nx - 2) // parts
+    copies = []
+    for p in range(parts):
+
+        def step(x, carry):
+            for t in range(1, ny // 8 - 1):
+                finish(post, None, None, x, t, stage)
+            return carry
+
+        low = 1 + p * size
+        lax.fori_loop(low, low + size, step, 0)
+        copies.append(send_out(stage, out_hbm, sem.at[p], low, size, 8, ny - 16))
+    for copy in copies:
+        copy.wait()
 
 
 def last_kernel(post, *refs):
-    halos, (out_hbm, stage, hx, hy, sem) = refs[:8], refs[8:]
+    halos, (out_in, out_hbm, stage, hx, hy, sem) = refs[:8], refs[8:]
     nx, ny = post.shape[1], post.shape[2]
     mark_halos(*halos, hx, hy)
-
-    def body(x):
+    copies = []
+    for n, x in enumerate((0, nx - 1)):
         for t in range(ny // 8):
-            f, own, fluid = stream(post, hx, hy, x, t)
-            for i in range(NQ):
-                stage[i, x, pl.ds(8 * t, 8), :] = jnp.where(fluid, f[i], own[i] * (1.0 / MARK))
-
-    def step(x, carry):
-        body(x)
-        return carry
-
-    parts = sem.shape[0]
-    size = nx // parts
-    copies = []
+            finish(post, hx, hy, x, t, stage)
+        copies.append(send_out(stage, out_hbm, sem.at[n], x, 1, 0, ny))
+    parts = (sem.shape[0] - 2) // 2
+    size = (nx - 2) // parts
     for p in range(parts):
-        begin, end = p * size, (p + 1) * size
-        if p == 0:
-            body(0)
-            begin = 1
-        if p == parts - 1:
-            end -= 1
-        lax.fori_loop(begin, end, step, 0)
-        if p == parts - 1:
-            body(nx - 1)
-        at = pl.ds(p * size, size)
-        copies.append(pltpu.make_async_copy(stage.at[:, at], out_hbm.at[:, at], sem.at[p]))
-        copies[-1].start()
+
+        def step(x, carry):
+            for t in (0, ny // 8 - 1):
+                finish(post, None, hy, x, t, stage)
+            return carry
+
+        low = 1 + p * size
+        lax.fori_loop(low, low + size, step, 0)
+        for n, y in enumerate((0, ny - 8)):
+            copies.append(send_out(stage, out_hbm, sem.at[2 + 2 * p + n], low, size, y, 8))
     for copy in copies:
         copy.wait()
 
@@ -287,65 +322,91 @@
     state = pltpu.VMEM(populations.shape, f32)
     params = pltpu.CompilerParams(vmem_limit_bytes=24 << 20)
 
-    def faces(x_planes, y_planes):
-        shape_x = jax.ShapeDtypeStruct((x_planes, ny, nz), f32)
-        shape_y = jax.ShapeDtypeStruct((y_planes, nx, nz), f32)
-        return (shape_x, shape_x, shape_y, shape_y)
-
-    def exchange(x0, x1, yp, ym):
-        r0, r1 = swap(x0, "gx", 0), swap(x1, "gx", 1)
+    def kernel(body, name, out_shape, in_specs, out_specs=None, scratch=(), aliases={}):
+        return pl.pallas_call(
+            body,
+            out_shape=out_shape,
+            in_specs=in_specs,
+            out_specs=out_specs or (onchip,) * len(out_shape),
+            scratch_shapes=list(scratch),
+            input_output_aliases=aliases,
+            compiler_params=params,
+            cost_estimate=pl.CostEstimate(flops=1 << 24, bytes_accessed=1 << 22, transcendentals=0),
+            name=name,
+        )
+
+    def held(value):
+        return pltpu.with_memory_space_constraint(value, pltpu.VMEM)
+
+    def face_x(planes):
+        return jax.ShapeDtypeStruct((planes, ny, nz), f32)
+
+    def face_y(planes):
+        return jax.ShapeDtypeStruct((planes, nx, nz), f32)
+
+    def swap_x(x0, x1):
+        return swap(x0, "gx", 0), swap(x1, "gx", 1)
+
+    def swap_y(yp, ym, r0, r1):
         shape = jax.ShapeDtypeStruct(yp.shape, f32)
-        y0, y1 = pl.pallas_call(
-            corner_kernel,
-            out_shape=(shape, shape),
-            in_specs=[onchip] * 4,
-            out_specs=(onchip,) * 2,
-            compiler_params=params,
-            name="corners",
-        )(yp, ym, r0, r1)
-        return r0, r1, swap(y0, "gy", 0), swap(y1, "gy", 1)
-
-    post, *out = pl.pallas_call(
-        first_kernel,
-        out_shape=(state,) + faces(6, 8),
-        in_specs=[anywhere, anywhere],
-        out_specs=(onchip,) * 5,
-        scratch_shapes=[pltpu.VMEM((6, ny, nz), f32)] * 2 + [
-            pltpu.VMEM(solid.shape, jnp.int32),
-            pltpu.SemaphoreType.DMA((4,)),
-            pltpu.SemaphoreType.DMA,
-        ],
-        compiler_params=params,
-        name="first",
+        y0, y1 = kernel(corner_kernel, "corners", (shape,) * 2, [onchip] * 4)(yp, ym, r0, r1)
+        return swap(y0, "gy", 0), swap(y1, "gy", 1)
+
+    post, x0, x1, yp, ym = kernel(
+        first_edge_kernel,
+        "first_edge",
+        (state, face_x(6), face_x(6), face_y(8), face_y(8)),
+        [anywhere] * 2,
+        scratch=[pltpu.VMEM((6, ny, nz), f32)] * 2
+        + [pltpu.VMEM(solid.shape, jnp.int32), pltpu.SemaphoreType.DMA((4,))],
     )(
         pltpu.with_memory_space_constraint(populations, pltpu.HBM),
         pltpu.with_memory_space_constraint(solid, pltpu.HBM),
     )
-    halos = exchange(*out)
-    flags = halos
+    r0, r1 = swap_x(x0, x1)
+    post, yp, ym = kernel(
+        first_inner_kernel,
+        "first_inner",
+        (state, face_y(8), face_y(8)),
+        [onchip] * 5,
+        aliases={2: 0, 3: 1, 4: 2},
+    )(held(populations), held(solid), held(post), yp, ym)
+    halos = flags = (r0, r1, *swap_y(yp, ym, r0, r1))
     marked = [pltpu.VMEM((2, 5, ny, nz), f32), pltpu.VMEM((2, 5, nx, nz), f32)]
     for _ in range(ITERS - 1):
-        post = pltpu.with_memory_space_constraint(post, pltpu.VMEM)
-        post, *out = pl.pallas_call(
-            middle_kernel,
-            out_shape=(state,) + faces(5, 5),
-            in_specs=[onchip] * 9,
-            out_specs=(onchip,) * 5,
-            scratch_shapes=[pltpu.VMEM((5, ny, nz), f32)] * 2 + marked,
-            compiler_params=params,
-            name="middle",
-        )(post, *halos, *flags)
-        halos = exchange(*out)
-    post = pltpu.with_memory_space_constraint(post, pltpu.VMEM)
-    return pl.pallas_call(
-        last_kernel,
-        out_shape=jax.ShapeDtypeStruct(populations.shape, f32),
-        in_specs=[onchip] * 9,
-        out_specs=anywhere,
-        scratch_shapes=[pltpu.VMEM(populations.shape, f32)] + marked + [pltpu.SemaphoreType.DMA((4,))],
-        compiler_params=params,
-        name="last",
-    )(post, *halos, *flags)
+        post = held(post)
+        (new,) = kernel(centre_kernel, "centre", (state,), [onchip])(post)
+        new, x0, x1, yp, ym, hy = kernel(
+            edge_kernel,
+            "edge",
+            (state, face_x(5), face_x(5), face_y(5), face_y(5), jax.ShapeDtypeStruct((2, 5, nx, nz), f32)),
+            [onchip] * 10,
+            scratch=[pltpu.VMEM((5, ny, nz), f32)] * 2 + marked[:1],
+            aliases={9: 0},
+        )(post, *halos, *flags, held(new))
+        r0, r1 = swap_x(x0, x1)
+        new, yp, ym = kernel(
+            rim_kernel,
+            "rim",
+            (state, face_y(5), face_y(5)),
+            [onchip] * 5,
+            aliases={2: 0, 3: 1, 4: 2},
+        )(post, hy, held(new), yp, ym)
+        halos = (r0, r1, *swap_y(yp, ym, r0, r1))
+        post = new
+    post = held(post)
+    whole = jax.ShapeDtypeStruct(populations.shape, f32)
+    stage = pltpu.VMEM(populations.shape, f32)
+    (out,) = kernel(
+        last_centre_kernel, "last_centre", (whole,), [onchip], (anywhere,),
+        scratch=[stage, pltpu.SemaphoreType.DMA((2,))],
+    )(post)
+    (out,) = kernel(
+        last_kernel, "last", (whole,), [onchip] * 9 + [anywhere], (anywhere,),
+        scratch=[stage] + marked + [pltpu.SemaphoreType.DMA((6,))],
+        aliases={9: 0},
+    )(post, *halos, *flags, out)
+    return out
 
 
 def solution(mesh):

time: 62.7 us -> 53.6 us (0.85)
  waiting for transfers between devices: 26 us -> 13.9 us
  Pallas kernels: 14 us -> 16.9 us
    ppermute x12, waiting for transfers between devices: 26 us -> 13.9 us  [swap(): return lax.ppermute(value, axis, pairs + [(b, a) for a, b in pairs])]
    pallas_call x7 -> x13, Pallas kernels: 14 us -> 16.9 us  [the longest x2 3.96 us: local(): new, = kernel(centre_kernel, 'centre', (state,), [onchip])(post)]
  transfers between devices with their start and end apart: 12 -> 12, of which waited for: 9 -> 6; matrix products, arithmetic and copies ran while one was open for 0% -> 0% of each run, Pallas kernels for 0% -> 23%
where the time goes in v1:
time: 53.6 us; the launch traced here: 53.5 us
  starting transfers between devices  22.5 us (42%)
  Pallas kernels  16.9 us (32%)
  waiting for transfers between devices  13.9 us (26%)
    ppermute x12, starting transfers between devices, swap(): return lax.ppermute(value, axis, pairs + [(b, a) for a, b in pairs])  22.5 us
    ppermute x12, waiting for transfers between devices, swap(): return lax.ppermute(value, axis, pairs + [(b, a) for a, b in pairs])  13.9 us
    pallas_call x2, Pallas kernels, local(): new, = kernel(centre_kernel, 'centre', (state,), [onchip])(post)  3.96 us
    pallas_call x2, Pallas kernels, local(): kernel(rim_kernel, 'rim', (state, face_y(5), face_y(5)), [onchip] * 5, al...  3.96 us
    pallas_call x1, Pallas kernels, local(): kernel(last_kernel, 'last', (whole,), [onchip] * 9 + [anywhere], (anywher...  2.59 us
    pallas_call x1, Pallas kernels, local(): kernel(last_centre_kernel, 'last_centre', (whole,), [onchip], (anywhere,)...  2.35 us
    pallas_call x1, Pallas kernels, local(): kernel(first_inner_kernel, 'first_inner', (state, face_y(8), face_y(8)),...  1.81 us
    pallas_call x1, Pallas kernels, local(): kernel(first_edge_kernel, 'first_edge', (state, face_x(6), face_x(6), fac...  1.45 us
  transfers between devices with their start and end apart: 12, of which 6 were waited for; matrix products, arithmetic and copies ran while one was open for 0% of the time, Pallas kernels for 23%

profile of v1, /device:TPU:0, one launch (start us, length us, event | category | flops | bytes accessed | tf_op | source)
XLA Modules:
  0.0 53.5 jit_solution(7396826457037186598)
XLA Ops:
  0.0 0.0 copy-start.1
  0.0 0.0 copy-start
  0.0 1.4 %first_edge.1 = (f32[19,16,32,128]{3,2,1,0:T(8,128)S(1)}, f32[6,32,128]{2,1,0:T(8,128)S(1)}, f32[6,32,128]{2,1,0:T(8,128)S(1)}, f32[8,16,128]{2,1,0:T(8,128)S(1)}, f32[8,16,128]{2,1,0:T(8,128)S(1)}) custom-call(f32[19,16,32,128]{3,2,1,0:T(8,128)} %f_ref.1, s32[16,32,128]{2,1,0:T(8,128)} %solid.1), custom_call_target="tpu_custom_call" | custom-call | flops 16777216 | bytes 4194304 | tf_op jit(solution)/shard_map/first_edge/pallas_call | solution.py:355
  1.5 0.1 collective-permute-start
  1.6 4.6 %collective-permute-start.1 = (f32[6,32,128]{2,1,0:T(8,128)S(1)}, f32[6,32,128]{2,1,0:T(8,128)S(1)}, u32[]{:S(2)}, u32[]{:S(2)}) collective-permute-start(f32[6,32,128]{2,1,0:T(8,128)S(1)} %get-tuple-element.42), channel_id=1, source_target_pairs={{8,16},{24,32},{40,48},{56,64},{72,80},{88,96},{104,112},{120,0},{... | collective-permute-start | bytes 294920 | tf_op jit(solution)/shard_map/ppermute | solution.py:314
  6.1 0.0 copy-done.1
  6.1 0.0 copy-done
  6.1 1.8 %first_inner.1 = (f32[19,16,32,128]{3,2,1,0:T(8,128)S(1)}, f32[8,16,128]{2,1,0:T(8,128)S(1)}, f32[8,16,128]{2,1,0:T(8,128)S(1)}) custom-call(f32[19,16,32,128]{3,2,1,0:T(8,128)S(1)} %copy-done, s32[16,32,128]{2,1,0:T(8,128)S(1)} %copy-done.1, ...), custom_call_target="tpu_custom_call", output_to_operand_aliasing={{0}: (2, {}), {1}: (3, {}), {2}: (4, {})} | custom-call | flops 16777216 | bytes 4194304 | tf_op jit(solution)/shard_map/first_inner/pallas_call | solution.py:367
  8.0 0.0 collective-permute-done.r0.refs_0_.refs_4_
  8.0 0.5 collective-permute-done.1.r1.refs_1_.refs_5_
  8.5 3.7 %collective-permute-start.2 = (f32[8,16,128]{2,1,0:T(8,128)S(1)}, f32[8,16,128]{2,1,0:T(8,128)S(1)}, u32[]{:S(2)}, u32[]{:S(2)}) collective-permute-start(f32[8,16,128]{2,1,0:T(8,128)S(1)} %get-tuple-element.45), channel_id=1, source_target_pairs={{0,1},{2,3},{4,5},{6,7},{1,0},{3,2},{5,4},{7,6},{8,9},{10,11},{12,... | collective-permute-start | bytes 196616 | tf_op jit(solution)/shard_map/ppermute | solution.py:314
  12.1 2.3 %collective-permute-start.3 = (f32[8,16,128]{2,1,0:T(8,128)S(1)}, f32[8,16,128]{2,1,0:T(8,128)S(1)}, u32[]{:S(2)}, u32[]{:S(2)}) collective-permute-start(f32[8,16,128]{2,1,0:T(8,128)S(1)} %get-tuple-element.46), channel_id=1, source_target_pairs={{1,2},{3,4},{5,6},{7,0},{2,1},{4,3},{6,5},{0,7},{9,10},{11,12},{13... | collective-permute-start | bytes 196616 | tf_op jit(solution)/shard_map/ppermute | solution.py:314
  14.4 2.0 %centre.2.refs_8_ = f32[19,16,32,128]{3,2,1,0:T(8,128)S(1)} custom-call(f32[19,16,32,128]{3,2,1,0:T(8,128)S(1)} %get-tuple-element.40.post), custom_call_target="tpu_custom_call" | custom-call | flops 16777216 | bytes 4194304 | tf_op jit(solution)/shard_map/centre/pallas_call | solution.py:378
  16.4 0.0 collective-permute-done.2.refs_2_.refs_6_
  16.4 3.6 %collective-permute-done.3.refs_3_.refs_7_ = f32[8,16,128]{2,1,0:T(8,128)S(1)} collective-permute-done((f32[8,16,128]{2,1,0:T(8,128)S(1)}, f32[8,16,128]{2,1,0:T(8,128)S(1)}, u32[]{:S(2)}, u32[]{:S(2)}) %collective-permute-start.3) | collective-permute-done | bytes 65568 | tf_op jit(solution)/shard_map/ppermute | solution.py:314
  20.0 0.4 edge.2
  20.4 0.1 collective-permute-start.4
  20.5 1.9 %collective-permute-start.5 = (f32[5,32,128]{2,1,0:T(8,128)S(1)}, f32[5,32,128]{2,1,0:T(8,128)S(1)}, u32[]{:S(2)}, u32[]{:S(2)}) collective-permute-start(f32[5,32,128]{2,1,0:T(8,128)S(1)} %get-tuple-element.53), channel_id=1, source_target_pairs={{8,16},{24,32},{40,48},{56,64},{72,80},{88,96},{104,112},{120,0},{... | collective-permute-start | bytes 245768 | tf_op jit(solution)/shard_map/ppermute | solution.py:314
  22.4 2.0 %rim.2 = (f32[19,16,32,128]{3,2,1,0:T(8,128)S(1)}, f32[5,16,128]{2,1,0:T(8,128)S(1)}, f32[5,16,128]{2,1,0:T(8,128)S(1)}) custom-call(f32[19,16,32,128]{3,2,1,0:T(8,128)S(1)} %get-tuple-element.40.post, f32[2,5,16,128]{3,2,1,0:T(8,128)S(1)} %get-tuple-element.47.hy, ...), custom_call_target="tpu_custom_call", output_to_operand_aliasing={{0}: (2, {}), {1}: (3, {}), {2}: (4, {})} | custom-call | flops 16777216 | bytes 4194304 | tf_op jit(solution)/shard_map/rim/pallas_call | solution.py:388
  24.4 0.0 collective-permute-done.4.r0.refs_0_
  24.4 2.2 %collective-permute-done.5.r1.refs_1_ = f32[5,32,128]{2,1,0:T(8,128)S(1)} collective-permute-done((f32[5,32,128]{2,1,0:T(8,128)S(1)}, f32[5,32,128]{2,1,0:T(8,128)S(1)}, u32[]{:S(2)}, u32[]{:S(2)}) %collective-permute-start.5) | collective-permute-done | bytes 81952 | tf_op jit(solution)/shard_map/ppermute | solution.py:314
  26.6 0.1 collective-permute-start.6
  26.7 4.5 %collective-permute-start.7 = (f32[5,16,128]{2,1,0:T(8,128)S(1)}, f32[5,16,128]{2,1,0:T(8,128)S(1)}, u32[]{:S(2)}, u32[]{:S(2)}) collective-permute-start(f32[5,16,128]{2,1,0:T(8,128)S(1)} %get-tuple-element.57), channel_id=1, source_target_pairs={{1,2},{3,4},{5,6},{7,0},{2,1},{4,3},{6,5},{0,7},{9,10},{11,12},{13... | collective-permute-start | bytes 122888 | tf_op jit(solution)/shard_map/ppermute | solution.py:314
  31.2 2.0 %centre.3.refs_8_ = f32[19,16,32,128]{3,2,1,0:T(8,128)S(1)} custom-call(f32[19,16,32,128]{3,2,1,0:T(8,128)S(1)} %get-tuple-element.51.post), custom_call_target="tpu_custom_call" | custom-call | flops 16777216 | bytes 4194304 | tf_op jit(solution)/shard_map/centre/pallas_call | solution.py:378
  33.1 0.0 collective-permute-done.6.refs_2_
  33.2 1.2 %collective-permute-done.7.refs_3_ = f32[5,16,128]{2,1,0:T(8,128)S(1)} collective-permute-done((f32[5,16,128]{2,1,0:T(8,128)S(1)}, f32[5,16,128]{2,1,0:T(8,128)S(1)}, u32[]{:S(2)}, u32[]{:S(2)}) %collective-permute-start.7) | collective-permute-done | bytes 40992 | tf_op jit(solution)/shard_map/ppermute | solution.py:314
  34.4 0.4 edge.3
  34.8 0.1 collective-permute-start.8
  34.9 0.7 %collective-permute-start.9 = (f32[5,32,128]{2,1,0:T(8,128)S(1)}, f32[5,32,128]{2,1,0:T(8,128)S(1)}, u32[]{:S(2)}, u32[]{:S(2)}) collective-permute-start(f32[5,32,128]{2,1,0:T(8,128)S(1)} %get-tuple-element.64), channel_id=1, source_target_pairs={{8,16},{24,32},{40,48},{56,64},{72,80},{88,96},{104,112},{120,0},{... | collective-permute-start | bytes 245768 | tf_op jit(solution)/shard_map/ppermute | solution.py:314
  35.6 2.0 %rim.3 = (f32[19,16,32,128]{3,2,1,0:T(8,128)S(1)}, f32[5,16,128]{2,1,0:T(8,128)S(1)}, f32[5,16,128]{2,1,0:T(8,128)S(1)}) custom-call(f32[19,16,32,128]{3,2,1,0:T(8,128)S(1)} %get-tuple-element.51.post, f32[2,5,16,128]{3,2,1,0:T(8,128)S(1)} %get-tuple-element.58.hy, ...), custom_call_target="tpu_custom_call", output_to_operand_aliasing={{0}: (2, {}), {1}: (3, {}), {2}: (4, {})} | custom-call | flops 16777216 | bytes 4194304 | tf_op jit(solution)/shard_map/rim/pallas_call | solution.py:388
  37.6 0.0 collective-permute-done.8.r0.refs_0_
  37.6 3.4 %collective-permute-done.9.r1.refs_1_ = f32[5,32,128]{2,1,0:T(8,128)S(1)} collective-permute-done((f32[5,32,128]{2,1,0:T(8,128)S(1)}, f32[5,32,128]{2,1,0:T(8,128)S(1)}, u32[]{:S(2)}, u32[]{:S(2)}) %collective-permute-start.9) | collective-permute-done | bytes 81952 | tf_op jit(solution)/shard_map/ppermute | solution.py:314
  41.0 2.3 %collective-permute-start.10 = (f32[5,16,128]{2,1,0:T(8,128)S(1)}, f32[5,16,128]{2,1,0:T(8,128)S(1)}, u32[]{:S(2)}, u32[]{:S(2)}) collective-permute-start(f32[5,16,128]{2,1,0:T(8,128)S(1)} %get-tuple-element.67), channel_id=1, source_target_pairs={{0,1},{2,3},{4,5},{6,7},{1,0},{3,2},{5,4},{7,6},{8,9},{10,11},{12,... | collective-permute-start | bytes 122888 | tf_op jit(solution)/shard_map/ppermute | solution.py:314
  43.3 2.3 %collective-permute-start.11 = (f32[5,16,128]{2,1,0:T(8,128)S(1)}, f32[5,16,128]{2,1,0:T(8,128)S(1)}, u32[]{:S(2)}, u32[]{:S(2)}) collective-permute-start(f32[5,16,128]{2,1,0:T(8,128)S(1)} %get-tuple-element.68), channel_id=1, source_target_pairs={{1,2},{3,4},{5,6},{7,0},{2,1},{4,3},{6,5},{0,7},{9,10},{11,12},{13... | collective-permute-start | bytes 122888 | tf_op jit(solution)/shard_map/ppermute | solution.py:314
  45.5 2.3 %last_centre.1.refs_8_ = f32[19,16,32,128]{3,2,1,0:T(8,128)} custom-call(f32[19,16,32,128]{3,2,1,0:T(8,128)S(1)} %get-tuple-element.62.post), custom_call_target="tpu_custom_call" | custom-call | flops 16777216 | bytes 4194304 | tf_op jit(solution)/shard_map/last_centre/pallas_call | solution.py:400
  47.9 0.0 collective-permute-done.10.refs_2_
  47.9 3.0 %collective-permute-done.11.refs_3_ = f32[5,16,128]{2,1,0:T(8,128)S(1)} collective-permute-done((f32[5,16,128]{2,1,0:T(8,128)S(1)}, f32[5,16,128]{2,1,0:T(8,128)S(1)}, u32[]{:S(2)}, u32[]{:S(2)}) %collective-permute-start.11) | collective-permute-done | bytes 40992 | tf_op jit(solution)/shard_map/ppermute | solution.py:314
  50.9 2.6 %last.1 = f32[19,16,32,128]{3,2,1,0:T(8,128)} custom-call(f32[19,16,32,128]{3,2,1,0:T(8,128)S(1)} %get-tuple-element.62.post, f32[5,32,128]{2,1,0:T(8,128)S(1)} %collective-permute-done.8.r0.refs_0_, f32[5,32,128]{2,1,0:T(8,128)S(1)} %collective-permute-done.9.r1.refs_1_, ...), custom_call_target="tpu_custom_call", output_to_operand_aliasing={{}: (9, {})} | custom-call | flops 16777216 | bytes 4194304 | tf_op jit(solution)/shard_map/last/pallas_call | solution.py:404
  (3 shorter events, 0.1 us)
Async XLA Ops:
  0.0 6.1 %copy-start.1 = (s32[16,32,128]{2,1,0:T(8,128)S(1)}, s32[16,32,128]{2,1,0:T(8,128)}, u32[]{:S(2)}) copy-start(s32[16,32,128]{2,1,0:T(8,128)} %solid.1) | copy-start | bytes 786436
  0.0 6.1 %copy-start = (f32[19,16,32,128]{3,2,1,0:T(8,128)S(1)}, f32[19,16,32,128]{3,2,1,0:T(8,128)}, u32[]{:S(2)}) copy-start(f32[19,16,32,128]{3,2,1,0:T(8,128)} %f_ref.1) | copy-start | bytes 14942212
  1.5 6.5 %collective-permute-start = (f32[6,32,128]{2,1,0:T(8,128)S(1)}, f32[6,32,128]{2,1,0:T(8,128)S(1)}, u32[]{:S(2)}, u32[]{:S(2)}) collective-permute-start(f32[6,32,128]{2,1,0:T(8,128)S(1)} %get-tuple-element.41), channel_id=1, source_target_pairs={{0,8},{16,24},{32,40},{48,56},{64,72},{80,88},{96,104},{112,120},{... | collective-permute-start | bytes 294920 | tf_op jit(solution)/shard_map/ppermute | solution.py:314
  1.6 6.9 %collective-permute-start.1 = (f32[6,32,128]{2,1,0:T(8,128)S(1)}, f32[6,32,128]{2,1,0:T(8,128)S(1)}, u32[]{:S(2)}, u32[]{:S(2)}) collective-permute-start(f32[6,32,128]{2,1,0:T(8,128)S(1)} %get-tuple-element.42), channel_id=1, source_target_pairs={{8,16},{24,32},{40,48},{56,64},{72,80},{88,96},{104,112},{120,0},{... | collective-permute-start | bytes 294920 | tf_op jit(solution)/shard_map/ppermute | solution.py:314
  8.5 7.9 %collective-permute-start.2 = (f32[8,16,128]{2,1,0:T(8,128)S(1)}, f32[8,16,128]{2,1,0:T(8,128)S(1)}, u32[]{:S(2)}, u32[]{:S(2)}) collective-permute-start(f32[8,16,128]{2,1,0:T(8,128)S(1)} %get-tuple-element.45), channel_id=1, source_target_pairs={{0,1},{2,3},{4,5},{6,7},{1,0},{3,2},{5,4},{7,6},{8,9},{10,11},{12,... | collective-permute-start | bytes 196616 | tf_op jit(solution)/shard_map/ppermute | solution.py:314
  12.1 7.9 %collective-permute-start.3 = (f32[8,16,128]{2,1,0:T(8,128)S(1)}, f32[8,16,128]{2,1,0:T(8,128)S(1)}, u32[]{:S(2)}, u32[]{:S(2)}) collective-permute-start(f32[8,16,128]{2,1,0:T(8,128)S(1)} %get-tuple-element.46), channel_id=1, source_target_pairs={{1,2},{3,4},{5,6},{7,0},{2,1},{4,3},{6,5},{0,7},{9,10},{11,12},{13... | collective-permute-start | bytes 196616 | tf_op jit(solution)/shard_map/ppermute | solution.py:314
  20.4 4.0 %collective-permute-start.4 = (f32[5,32,128]{2,1,0:T(8,128)S(1)}, f32[5,32,128]{2,1,0:T(8,128)S(1)}, u32[]{:S(2)}, u32[]{:S(2)}) collective-permute-start(f32[5,32,128]{2,1,0:T(8,128)S(1)} %get-tuple-element.52), channel_id=1, source_target_pairs={{0,8},{16,24},{32,40},{48,56},{64,72},{80,88},{96,104},{112,120},{... | collective-permute-start | bytes 245768 | tf_op jit(solution)/shard_map/ppermute | solution.py:314
  20.5 6.1 %collective-permute-start.5 = (f32[5,32,128]{2,1,0:T(8,128)S(1)}, f32[5,32,128]{2,1,0:T(8,128)S(1)}, u32[]{:S(2)}, u32[]{:S(2)}) collective-permute-start(f32[5,32,128]{2,1,0:T(8,128)S(1)} %get-tuple-element.53), channel_id=1, source_target_pairs={{8,16},{24,32},{40,48},{56,64},{72,80},{88,96},{104,112},{120,0},{... | collective-permute-start | bytes 245768 | tf_op jit(solution)/shard_map/ppermute | solution.py:314
  26.6 6.5 %collective-permute-start.6 = (f32[5,16,128]{2,1,0:T(8,128)S(1)}, f32[5,16,128]{2,1,0:T(8,128)S(1)}, u32[]{:S(2)}, u32[]{:S(2)}) collective-permute-start(f32[5,16,128]{2,1,0:T(8,128)S(1)} %get-tuple-element.56), channel_id=1, source_target_pairs={{0,1},{2,3},{4,5},{6,7},{1,0},{3,2},{5,4},{7,6},{8,9},{10,11},{12,... | collective-permute-start | bytes 122888 | tf_op jit(solution)/shard_map/ppermute | solution.py:314
  26.7 7.7 %collective-permute-start.7 = (f32[5,16,128]{2,1,0:T(8,128)S(1)}, f32[5,16,128]{2,1,0:T(8,128)S(1)}, u32[]{:S(2)}, u32[]{:S(2)}) collective-permute-start(f32[5,16,128]{2,1,0:T(8,128)S(1)} %get-tuple-element.57), channel_id=1, source_target_pairs={{1,2},{3,4},{5,6},{7,0},{2,1},{4,3},{6,5},{0,7},{9,10},{11,12},{13... | collective-permute-start | bytes 122888 | tf_op jit(solution)/shard_map/ppermute | solution.py:314
  34.8 2.8 %collective-permute-start.8 = (f32[5,32,128]{2,1,0:T(8,128)S(1)}, f32[5,32,128]{2,1,0:T(8,128)S(1)}, u32[]{:S(2)}, u32[]{:S(2)}) collective-permute-start(f32[5,32,128]{2,1,0:T(8,128)S(1)} %get-tuple-element.63), channel_id=1, source_target_pairs={{0,8},{16,24},{32,40},{48,56},{64,72},{80,88},{96,104},{112,120},{... | collective-permute-start | bytes 245768 | tf_op jit(solution)/shard_map/ppermute | solution.py:314
  34.9 6.1 %collective-permute-start.9 = (f32[5,32,128]{2,1,0:T(8,128)S(1)}, f32[5,32,128]{2,1,0:T(8,128)S(1)}, u32[]{:S(2)}, u32[]{:S(2)}) collective-permute-start(f32[5,32,128]{2,1,0:T(8,128)S(1)} %get-tuple-element.64), channel_id=1, source_target_pairs={{8,16},{24,32},{40,48},{56,64},{72,80},{88,96},{104,112},{120,0},{... | collective-permute-start | bytes 245768 | tf_op jit(solution)/shard_map/ppermute | solution.py:314
  41.0 6.9 %collective-permute-start.10 = (f32[5,16,128]{2,1,0:T(8,128)S(1)}, f32[5,16,128]{2,1,0:T(8,128)S(1)}, u32[]{:S(2)}, u32[]{:S(2)}) collective-permute-start(f32[5,16,128]{2,1,0:T(8,128)S(1)} %get-tuple-element.67), channel_id=1, source_target_pairs={{0,1},{2,3},{4,5},{6,7},{1,0},{3,2},{5,4},{7,6},{8,9},{10,11},{12,... | collective-permute-start | bytes 122888 | tf_op jit(solution)/shard_map/ppermute | solution.py:314
  43.3 7.6 %collective-permute-start.11 = (f32[5,16,128]{2,1,0:T(8,128)S(1)}, f32[5,16,128]{2,1,0:T(8,128)S(1)}, u32[]{:S(2)}, u32[]{:S(2)}) collective-permute-start(f32[5,16,128]{2,1,0:T(8,128)S(1)} %get-tuple-element.68), channel_id=1, source_target_pairs={{1,2},{3,4},{5,6},{7,0},{2,1},{4,3},{6,5},{0,7},{9,10},{11,12},{13... | collective-permute-start | bytes 122888 | tf_op jit(solution)/shard_map/ppermute | solution.py:314
